TPU v7x, 32 devices: a whole 2x2x4 slice. The times are simulated.
32 devices in a mesh: groups: 2 (over x), ctx: 16 (over z, y, core).
Axes of the slice: x: 2, y: 2, z: 4, core: 2. Of those that a mesh axis runs over, the one named last changes fastest.
Arguments:
- raster_tokens: bfloat16 [4096, 1024], P(('groups', 'ctx')), parts along dimension 0, may hold values from -45 to 45
- hilbert_perm: int32 [4096], P(('groups', 'ctx')), parts along dimension 0, may hold values from 0 to 2047, as said below
- neighbors: int32 [32, 5], P(('groups', 'ctx')), parts along dimension 0, may hold values from 0 to 15, as said below
- neighbor_counts: int32 [32], P(('groups', 'ctx')), parts along dimension 0, may hold values from 1 to 5, as said below
- norm_gain: float32 [1024], replicated, may hold values from 0.1 to 1.9
- w_qkv: bfloat16 [1024, 3072], replicated, may hold values from -0.8125 to 0.8125
- w_out: bfloat16 [1024, 1024], replicated, may hold values from -0.5 to 0.5
- cotangent: bfloat16 [4096, 1024], P(('groups', 'ctx')), parts along dimension 0, may hold values from -6 to 6
Outputs:
- layer_out: bfloat16 [4096, 1024], P(('groups', 'ctx')), parts along dimension 0
- grad_tokens: bfloat16 [4096, 1024], P(('groups', 'ctx')), parts along dimension 0
- grad_w_out: float32 [2048, 1024], P(('groups', 'ctx')), parts along dimension 0
- grad_gain: float32 [2048], P('groups'), parts along dimension 0
There are 2 independent parts, one for each index of `groups`. A program takes and returns all parts, laid end to end along the dimension named above; an argument that names none is the same for every part. Nothing has to cross between parts.
Inputs may be any that keep to these rules, and one draw needn't show every extreme that they name: `hilbert_perm`: A permutation. Every 128 consecutive positions of the Hilbert order take exactly 8 tokens from every 128 consecutive raster tokens. `neighbors`: row b starts with b, followed by distinct blocks other than b at a distance of at most 4; entries from slot neighbor_counts[b] on equal b. `neighbor_counts`: the block itself is counted.
All inputs are finite; a program needn't handle non-finite values.
Results may differ from a plain program's by a relative error of at most 0.02.
The roundings to bfloat16 on the way count: a program that leaves them out, or rounds other values in their place, can miss the bound.
Values may be sent and summed in bfloat16 or wider, within the bound.
No kernel may reach another device: no remote copies, remote signals or barrier semaphores. Data moves between devices by JAX's collectives and lax.ppermute only.
A program may use at most 128 MiB of HBM per device.

v0:
```python
import jax
import jax.numpy as jnp
from jax import lax
from jax.sharding import PartitionSpec as P

HEADS = 16
BLOCK = 128
REACH = 4
EPS = 1e-06
FAR = -1e30


def from_behind(block, axis, distance):
    devices = range(lax.axis_size(axis))
    route = [(i - distance, i) for i in devices if i - distance in devices]
    return lax.ppermute(block, axis, route)


def softmax_probs(heads_q, heads_k, counts, score_scale):
    scores = (
        jnp.einsum("sqhd,skhd->shqk", heads_q, heads_k, preferred_element_type=jnp.float32)
        * score_scale
    )
    slot_of = jnp.arange(heads_k.shape[1]) // BLOCK
    usable = slot_of[None, :] < counts[:, None]
    scores = jnp.where(usable[:, None, None, :], scores, FAR)
    row_max = jnp.max(scores, axis=-1, keepdims=True)
    shifted = jnp.exp(scores - row_max)
    return shifted / jnp.sum(shifted, axis=-1, keepdims=True)


def per_device(
    raster_tokens, hilbert_perm, neighbors, neighbor_counts, norm_gain, w_qkv, w_out, cotangent
):
    axis_size = lax.axis_size("ctx")
    my_index = lax.axis_index("ctx")
    tok_rows, model_width = raster_tokens.shape
    per_peer = tok_rows // axis_size
    per_dev = tok_rows // BLOCK
    reach_dev = (REACH + per_dev - 1) // per_dev
    head_dim = model_width // HEADS
    score_scale = head_dim ** (-0.5)
    norm_scale = (tok_rows * axis_size) ** (-0.5)
    source_dev = hilbert_perm // tok_rows
    local_row = hilbert_perm % tok_rows
    sorted_rows = jnp.argsort(source_dev, stable=True)
    wanted = local_row[sorted_rows].reshape(axis_size, per_peer)
    requested = lax.all_to_all(wanted, "ctx", split_axis=0, concat_axis=0, tiled=True)
    requested_flat = requested.reshape(-1)
    outgoing = raster_tokens[requested_flat].reshape(axis_size, per_peer, model_width)
    arrived = lax.all_to_all(outgoing, "ctx", split_axis=0, concat_axis=0, tiled=True)
    ordered = (
        jnp.zeros_like(raster_tokens).at[sorted_rows].set(arrived.reshape(tok_rows, model_width))
    )
    ordered_f = ordered.astype(jnp.float32)
    inv_rms = lax.rsqrt(jnp.mean(ordered_f * ordered_f, axis=-1, keepdims=True) + EPS)
    normed = (ordered_f * inv_rms * norm_gain).astype(jnp.bfloat16)
    projected = jnp.dot(normed, w_qkv, preferred_element_type=jnp.float32).astype(jnp.bfloat16)
    queries = projected[:, :model_width]
    keys_vals = projected[:, model_width:]
    kv_weight = w_qkv[:, model_width:]
    from_lower = []
    from_upper = []
    carry_low = normed
    carry_high = normed
    for distance in range(reach_dev):
        carry_low = from_behind(carry_low, "ctx", 1)
        carry_high = from_behind(carry_high, "ctx", -1)
        from_lower.append(carry_low)
        from_upper.append(carry_high)
    remote_low = [
        jnp.dot(remote_piece, kv_weight, preferred_element_type=jnp.float32).astype(jnp.bfloat16)
        for remote_piece in from_lower
    ]
    remote_high = [
        jnp.dot(remote_piece, kv_weight, preferred_element_type=jnp.float32).astype(jnp.bfloat16)
        for remote_piece in from_upper
    ]
    window = jnp.concatenate(remote_low[::-1] + [keys_vals] + remote_high, axis=0)
    window_blocks = window.reshape(-1, BLOCK, 2 * model_width)
    slot_index = neighbors - (my_index - reach_dev) * per_dev
    gathered = window_blocks[slot_index].reshape(per_dev, -1, 2 * model_width)
    heads_k = gathered[:, :, :model_width].reshape(per_dev, -1, HEADS, head_dim)
    heads_v = gathered[:, :, model_width:].reshape(per_dev, -1, HEADS, head_dim)
    heads_q = queries.reshape(per_dev, BLOCK, HEADS, head_dim)
    weights_f = softmax_probs(heads_q, heads_k, neighbor_counts, score_scale)
    probs_b = weights_f.astype(jnp.bfloat16)
    attended = jnp.einsum("shqk,skhd->sqhd", probs_b, heads_v, preferred_element_type=jnp.float32)
    attended = attended.reshape(tok_rows, model_width).astype(jnp.bfloat16)
    projected_out = jnp.dot(attended, w_out, preferred_element_type=jnp.float32)
    layer_out = (ordered_f + projected_out).astype(jnp.bfloat16)
    grad_w_out = None
    d_attended = jnp.dot(cotangent, w_out.T, preferred_element_type=jnp.float32).astype(
        jnp.bfloat16
    )
    d_heads = d_attended.reshape(per_dev, BLOCK, HEADS, head_dim)
    d_probs = jnp.einsum("sqhd,skhd->shqk", d_heads, heads_v, preferred_element_type=jnp.float32)
    row_dots = jnp.sum(d_probs * weights_f, axis=-1, keepdims=True)
    d_scores = (weights_f * (d_probs - row_dots) * score_scale).astype(jnp.bfloat16)
    d_query = jnp.einsum("shqk,skhd->sqhd", d_scores, heads_k, preferred_element_type=jnp.float32)
    d_query = d_query.reshape(tok_rows, model_width).astype(jnp.bfloat16)
    d_keys = jnp.einsum("shqk,sqhd->skhd", d_scores, heads_q, preferred_element_type=jnp.float32)
    d_vals = jnp.einsum("shqk,sqhd->skhd", probs_b, d_heads, preferred_element_type=jnp.float32)
    contrib = jnp.concatenate(
        [d_keys.reshape(-1, BLOCK, model_width), d_vals.reshape(-1, BLOCK, model_width)], axis=-1
    )
    summed = jnp.zeros(window_blocks.shape, jnp.float32).at[slot_index.reshape(-1)].add(contrib)
    partials = summed.astype(jnp.bfloat16)
    accum = partials[reach_dev].astype(jnp.float32)
    for distance in range(1, reach_dev + 1):
        accum = accum + from_behind(partials[reach_dev + distance], "ctx", distance).astype(
            jnp.float32
        )
        accum = accum + from_behind(partials[reach_dev - distance], "ctx", -distance).astype(
            jnp.float32
        )
    d_kv = accum.astype(jnp.bfloat16)
    d_proj = jnp.concatenate([d_query, d_kv], axis=-1)
    d_normed = jnp.dot(d_proj, w_qkv.T, preferred_element_type=jnp.float32)
    gain_term = jnp.sum(d_normed * ordered_f * inv_rms, axis=0)
    grad_gain = lax.psum(gain_term, "ctx") * norm_scale
    scaled = d_normed * norm_gain
    d_ordered = (
        cotangent.astype(jnp.float32)
        + inv_rms * scaled
        - ordered_f * inv_rms**3 * jnp.mean(scaled * ordered_f, axis=-1, keepdims=True)
    )
    d_ordered = d_ordered.astype(jnp.bfloat16)
    leaving = d_ordered[sorted_rows].reshape(axis_size, per_peer, model_width)
    returned = lax.all_to_all(leaving, "ctx", split_axis=0, concat_axis=0, tiled=True)
    grad_tokens = (
        jnp.zeros_like(raster_tokens)
        .at[requested_flat]
        .set(returned.reshape(tok_rows, model_width))
    )
    grad_w_out = (
        lax.psum_scatter(
            lax.dot_general(
                attended, cotangent, (((0,), (0,)), ((), ())), preferred_element_type=jnp.float32
            ),
            "ctx",
            scatter_dimension=0,
            tiled=True,
        )
        * norm_scale
    )
    return (layer_out, grad_tokens, grad_w_out, grad_gain)


def solution(mesh):
    placed = (
        P(("groups", "ctx"), None),
        P(("groups", "ctx")),
        P(("groups", "ctx"), None),
        P(("groups", "ctx")),
        P(),
        P(),
        P(),
        P(("groups", "ctx"), None),
    )
    return jax.shard_map(
        per_device,
        mesh=mesh,
        in_specs=placed,
        out_specs=(
            P(("groups", "ctx"), None),
            P(("groups", "ctx"), None),
            P(("groups", "ctx"), None),
            P("groups"),
        ),
        check_vma=False,
    )
```

profile of v0, /device:TPU:0, one launch (start us, length us, event | category | flops | bytes accessed | tf_op | source)
XLA Modules:
  0.0 316.0 jit_solution(17017370256104363028)
XLA Ops:
  11.9 13.6 %all_to_all.19 = s32[16,1,8]{2,1,0:T(1,128)S(1)} all-to-all(s32[16,1,8]{2,1,0:T(1,128)S(1)} %bitcast.117), channel_id=1, replica_groups=mesh['groups'=2,'ctx'=16] {'ctx'}, dimensions={0} | all-to-all | bytes 1024 | tf_op jit(solution)/shard_map/all_to_all | solution.py:48
  28.9 12.6 %all_to_all.20 = bf16[16,8,1024]{2,1,0:T(8,128)(2,1)S(1)} all-to-all(bf16[16,8,1024]{2,1,0:T(8,128)(2,1)S(1)} %bitcast.109), channel_id=1, replica_groups=mesh['groups'=2,'ctx'=16] {'ctx'}, dimensions={0} | all-to-all | bytes 524288 | tf_op jit(solution)/shard_map/all_to_all | solution.py:51
  46.8 4.6 %collective-permute-start.1 = (bf16[128,1024]{1,0:T(8,128)(2,1)S(1)}, bf16[128,1024]{1,0:T(8,128)(2,1)}, u32[]{:S(2)}, u32[]{:S(2)}) collective-permute-start(bf16[128,1024]{1,0:T(8,128)(2,1)S(1)} %collective-permute-done), channel_id=1, source_target_pairs={{0,1},{1,2},{2,3},{3,4},{4,5},{5,6},{6,7},{7,8},{8,9},{9,10},{10,1... | collective-permute-start | bytes 786440 | tf_op jit(solution)/shard_map/ppermute | solution.py:16
  52.7 6.4 %collective-permute-start.2 = (bf16[128,1024]{1,0:T(8,128)(2,1)}, bf16[128,1024]{1,0:T(8,128)(2,1)}, u32[]{:S(2)}, u32[]{:S(2)}) collective-permute-start(bf16[128,1024]{1,0:T(8,128)(2,1)} %collective-permute-done.1), channel_id=1, source_target_pairs={{0,1},{1,2},{2,3},{3,4},{4,5},{5,6},{6,7},{7,8},{8,9},{9,10},{10,1... | collective-permute-start | bytes 786440 | tf_op jit(solution)/shard_map/ppermute | solution.py:16
  61.1 6.1 %collective-permute-start.3 = (bf16[128,1024]{1,0:T(8,128)(2,1)}, bf16[128,1024]{1,0:T(8,128)(2,1)}, u32[]{:S(2)}, u32[]{:S(2)}) collective-permute-start(bf16[128,1024]{1,0:T(8,128)(2,1)} %collective-permute-done.2), channel_id=1, source_target_pairs={{0,1},{1,2},{2,3},{3,4},{4,5},{5,6},{6,7},{7,8},{8,9},{9,10},{10,1... | collective-permute-start | bytes 786440 | tf_op jit(solution)/shard_map/ppermute | solution.py:16
  67.2 3.8 %convolution_convert_fusion = bf16[128,3072]{1,0:T(8,128)(2,1)S(1)} fusion(bf16[128,1024]{1,0:T(8,128)(2,1)S(1)} %fusion.60, bf16[1024,3072]{1,0:T(8,128)(2,1)} %param.13), kind=kOutput, calls=%fused_computation.16 | convolution fusion | flops 805699584 | bytes 7340032 | tf_op jit(solution)/shard_map/dot_general | solution.py:58
  73.2 3.1 fusion.24
  76.3 3.1 fusion.23
  90.5 4.7 %gather_fusion.2 = bf16[5,128,2048]{2,1,0:T(8,128)(2,1)} fusion(bf16[9,128,2048]{2,1,0:T(8,128)(2,1)} %bitcast.106, s32[1024]{0:T(1024)S(1)} %pad_clamp_fusion), kind=kCustom, calls=%fused_computation.2 | custom fusion | bytes 5242900 | tf_op jit(solution)/shard_map/gather | solution.py:82
  95.2 3.5 %fusion.89 = (bf16[1,640,1024]{2,1,0:T(8,128)(2,1)}, bf16[1,640,1024]{2,1,0:T(8,128)(2,1)}) fusion(bf16[1,640,2048]{2,1,0:T(8,128)(2,1)} %bitcast.103), kind=kLoop, calls=%fused_computation.138 | loop fusion | bytes 5242880 | tf_op jit(solution)/shard_map/slice | solution.py:83
  103.6 5.5 %fusion.90 = (f32[16,128]{1,0:T(8,128)S(1)}, f32[16,128,640]{2,1,0:T(8,128)}) fusion(pred[640]{0:T(1024)(128)(4,1)S(1)} %fusion.75, bf16[128,16,64]{0,2,1:T(8,128)(2,1)S(1)} %bitcast.114, bf16[640,16,64]{0,2,1:T(8,128)(2,1)} %bitcast.107), kind=kOutput, calls=%fused_computation.139 | convolution fusion | flops 173015680 | bytes 6824576 | tf_op jit(solution)/shard_map/sub | solution.py:28
  109.2 4.1 %fusion.31 = bf16[16,64,128]{2,1,0:T(8,128)(2,1)S(1)} fusion(bf16[640,16,64]{0,2,1:T(8,128)(2,1)} %bitcast.104, f32[16,128,640]{2,1,0:T(8,128)} %get-tuple-element.23, f32[16,128]{1,0:T(8,128)S(1)} %get-tuple-element.22), kind=kOutput, calls=%fused_computation.47 | convolution fusion | flops 170524672 | bytes 6823936 | tf_op jit(solution)/shard_map/shqk,skhd->sqhd/dot_general | solution.py:88
  117.0 4.6 %convolution_bitcast_fusion = f32[1,640,16,64]{1,3,2,0:T(8,128)} fusion(bf16[128,16,64]{0,2,1:T(8,128)(2,1)S(1)} %bitcast.112, f32[16,128,640]{2,1,0:T(8,128)} %get-tuple-element.23, f32[16,128]{1,0:T(8,128)S(1)} %get-tuple-element.22), kind=kOutput, calls=%fused_computation.42 | convolution fusion | flops 170393600 | bytes 8134656 | tf_op jit(solution)/shard_map/shqk,sqhd->skhd/dot_general | solution.py:103
  121.6 4.4 %reshape.226 = f32[5,128,1024]{1,0,2:T(8,128)} reshape(f32[1,640,16,64]{1,3,2,0:T(8,128)} %convolution_bitcast_fusion) | data formatting | bytes 5242880 | tf_op jit(solution)/shard_map/reshape | solution.py:105
  126.0 4.6 %fusion.91 = f32[16,128,640]{2,1,0:T(8,128)} fusion(bf16[128,16,64]{0,2,1:T(8,128)(2,1)S(1)} %bitcast.113, bf16[640,16,64]{0,2,1:T(8,128)(2,1)} %bitcast.105), kind=kOutput, calls=%fused_computation.140 | convolution fusion | flops 167772160 | bytes 6815744 | tf_op jit(solution)/shard_map/sqhd,skhd->shqk/dot_general | solution.py:97
  130.6 19.2 %fusion.25 = f32[1,640,16,64]{1,3,2,0:T(8,128)} fusion(bf16[128,16,64]{0,2,1:T(8,128)(2,1)S(1)} %bitcast.115, f32[16,128,640]{2,1,0:T(8,128)} %fusion.91, f32[16,128,640]{2,1,0:T(8,128)} %get-tuple-element.23, f32[16,128]{1,0:T(8,128)S(1)} %get-tuple-element.22), kind=kOutput, calls=%fused_computation.41 | convolution fusion | flops 176949888 | bytes 13377536 | tf_op jit(solution)/shard_map/shqk,sqhd->skhd/dot_general | solution.py:102
  149.9 4.4 %reshape.225 = f32[5,128,1024]{1,0,2:T(8,128)} reshape(f32[1,640,16,64]{1,3,2,0:T(8,128)} %fusion.25) | data formatting | bytes 5242880 | tf_op jit(solution)/shard_map/reshape | solution.py:105
  154.3 6.7 %pad_maximum_fusion = f32[5,128,2048]{1,0,2:T(8,128)} fusion(f32[5,128,1024]{1,0,2:T(8,128)} %reshape.226, f32[5,128,1024]{1,0,2:T(8,128)} %reshape.225), kind=kLoop, calls=%fused_computation.9 | loop fusion | flops 1310720 | bytes 10485760 | tf_op jit(solution)/shard_map/concatenate | solution.py:104
  161.0 7.9 %copy.30 = f32[5,128,2048]{2,1,0:T(8,128)} copy(f32[5,128,2048]{1,0,2:T(8,128)} %pad_maximum_fusion) | data formatting | bytes 10485760 | tf_op jit(solution)/shard_map/concatenate | solution.py:104
  168.9 4.8 %broadcast_in_dim.22 = f32[9,128,2048]{2,1,0:T(8,128)} broadcast(f32[]{:T(128)} %constant.63.clone.1), dimensions={} | broadcast | bytes 9437188 | tf_op jit(solution)/shard_map/broadcast_in_dim | solution.py:107
  173.7 11.9 %scatter_fusion = f32[9,128,2048]{2,1,0:T(8,128)} fusion(f32[9,128,2048]{2,1,0:T(8,128)} %broadcast_in_dim.22, s32[5]{0:T(128)S(1)} %fusion.81, f32[5,128,2048]{2,1,0:T(8,128)} %copy.30), kind=kCustom, calls=%fused_computation.5 | custom fusion | flops 1310720 | bytes 15728660 | tf_op jit(solution)/shard_map/scatter-add | solution.py:107
  185.7 4.4 %convert_element_type.137 = bf16[9,128,2048]{2,1,0:T(8,128)(2,1)S(1)} convert(f32[9,128,2048]{2,1,0:T(8,128)} %scatter_fusion) | non-fusion elementwise | flops 2359296 | bytes 14155776 | tf_op jit(solution)/shard_map/convert_element_type | solution.py:108
  193.8 5.4 %collective-permute-start.8 = (bf16[128,2048]{1,0:T(8,128)(2,1)S(1)}, bf16[128,2048]{1,0:T(8,128)(2,1)}, u32[]{:S(2)}, u32[]{:S(2)}) collective-permute-start(bf16[128,2048]{1,0:T(8,128)(2,1)S(1)} %get-tuple-element.8), channel_id=1, source_target_pairs={{0,1},{1,2},{2,3},{3,4},{4,5},{5,6},{6,7},{7,8},{8,9},{9,10},{10,1... | collective-permute-start | bytes 1572872 | tf_op jit(solution)/shard_map/ppermute | solution.py:16
  200.5 7.8 %collective-permute-start.14 = (bf16[128,2048]{1,0:T(8,128)(2,1)S(1)}, bf16[128,2048]{1,0:T(8,128)(2,1)}, u32[]{:S(2)}, u32[]{:S(2)}) collective-permute-start(bf16[128,2048]{1,0:T(8,128)(2,1)S(1)} %get-tuple-element.10), channel_id=1, source_target_pairs={{0,4},{1,5},{2,6},{3,7},{4,8},{5,9},{6,10},{7,11},{8,12},{9,13},{1... | collective-permute-start | bytes 1572872 | tf_op jit(solution)/shard_map/ppermute | solution.py:16
  209.8 6.8 %collective-permute-start.12 = (bf16[128,2048]{1,0:T(8,128)(2,1)}, bf16[128,2048]{1,0:T(8,128)(2,1)}, u32[]{:S(2)}, u32[]{:S(2)}) collective-permute-start(bf16[128,2048]{1,0:T(8,128)(2,1)} %get-tuple-element.12), channel_id=1, source_target_pairs={{0,3},{1,4},{2,5},{3,6},{4,7},{5,8},{6,9},{7,10},{8,11},{9,12},{10... | collective-permute-start | bytes 1572872 | tf_op jit(solution)/shard_map/ppermute | solution.py:16
  218.4 4.9 %collective-permute-start.10 = (bf16[128,2048]{1,0:T(8,128)(2,1)}, bf16[128,2048]{1,0:T(8,128)(2,1)}, u32[]{:S(2)}, u32[]{:S(2)}) collective-permute-start(bf16[128,2048]{1,0:T(8,128)(2,1)} %get-tuple-element.14), channel_id=1, source_target_pairs={{0,2},{1,3},{2,4},{3,5},{4,6},{5,7},{6,8},{7,9},{8,10},{9,11},{10,... | collective-permute-start | bytes 1572872 | tf_op jit(solution)/shard_map/ppermute | solution.py:16
  224.6 19.1 %fusion.34 = bf16[16,64,128]{2,1,0:T(8,128)(2,1)S(1)} fusion(bf16[640,16,64]{0,2,1:T(8,128)(2,1)} %bitcast.108, f32[16,128,640]{2,1,0:T(8,128)} %fusion.91, f32[16,128,640]{2,1,0:T(8,128)} %get-tuple-element.23, f32[16,128]{1,0:T(8,128)S(1)} %get-tuple-element.22), kind=kOutput, calls=%fused_computation.48 | convolution fusion | flops 177080960 | bytes 12066816 | tf_op jit(solution)/shard_map/shqk,skhd->sqhd/dot_general | solution.py:100
  245.8 9.2 %collective-permute-done.10 = bf16[128,2048]{1,0:T(8,128)(2,1)} collective-permute-done((bf16[128,2048]{1,0:T(8,128)(2,1)}, bf16[128,2048]{1,0:T(8,128)(2,1)}, u32[]{:S(2)}, u32[]{:S(2)}) %collective-permute-start.10) | collective-permute-done | bytes 524320 | tf_op jit(solution)/shard_map/ppermute | solution.py:16
  255.0 3.1 fusion.45
  258.0 5.1 %fusion.66 = (f32[1024]{0:T(1024)S(1)}, f32[128]{0:T(128)S(1)}, f32[128,1024]{1,0:T(8,128)S(1)}) fusion(bf16[128,1024]{1,0:T(8,128)(2,1)S(1)} %scatter_custom_fusion, f32[128]{0:T(128)S(1)} %get-tuple-element.19, f32[1024]{0:T(1024)S(1)} %copy-done.6, bf16[1024,3072]{1,0:T(8,128)(2,1)} %param.13, bf16[128,2048]{1,0:T(8,128)(2,1)S(1)} %fusion.45, ...), kind=kOutput, calls=%fused_computation.85 | convolution fusion | flops 807795584 | bytes 7873536 | tf_op jit(solution)/shard_map/dot_general | solution.py:119
  265.0 5.1 %all-to-all-start.2 = ((bf16[16,8,1024]{2,1,0:T(8,128)(2,1)}), bf16[16,8,1024]{2,1,0:T(8,128)(2,1)S(1)}, u32[]{:S(2)}, u32[]{:S(2)}) async-start(bf16[16,8,1024]{2,1,0:T(8,128)(2,1)} %bitcast.33), calls=%async_computation.2 | async-start | bytes 524288 | tf_op jit(solution)/shard_map/all_to_all | solution.py:130
  271.3 33.8 %psum.7 = f32[1024]{0:T(1024)S(1)} all-reduce(f32[1024]{0:T(1024)S(1)} %get-tuple-element.6), channel_id=1, replica_groups=mesh['groups'=2,'ctx'=16] {'ctx'}, use_global_device_ids=true, to_apply=%region_11.12 | all-reduce | flops 1024 | bytes 8192 | tf_op jit(solution)/shard_map/psum | solution.py:121
  (101 shorter events, 56.2 us)
Async XLA Ops:
  7.2 108.8 %copy-start = (bf16[1024,1024]{1,0:T(8,128)(2,1)S(1)}, bf16[1024,1024]{1,0:T(8,128)(2,1)}, u32[]{:S(2)}) copy-start(bf16[1024,1024]{1,0:T(8,128)(2,1)} %param.14) | copy-start | bytes 6291460
  7.2 51.9 %copy-start.11 = (s32[1,5]{1,0:T(1,128)S(1)}, s32[1,5]{1,0:T(1,128)}, u32[]{:S(2)}) copy-start(s32[1,5]{1,0:T(1,128)} %param.10) | copy-start | bytes 64
  7.2 300.3 %reduce-scatter.2.cloned.1.call-start = ((), (), s32[]{:S(2)}) async-start(), calls=%async_computation.4 | async-start | bytes 4456448 | tf_op jit(solution)/shard_map/reduce_scatter | solution.py:137
  43.7 3.1 collective-permute-start
  45.5 5.9 %collective-permute-start.4 = (bf16[128,1024]{1,0:T(8,128)(2,1)S(1)}, bf16[128,1024]{1,0:T(8,128)(2,1)S(1)}, u32[]{:S(2)}, u32[]{:S(2)}) collective-permute-start(bf16[128,1024]{1,0:T(8,128)(2,1)S(1)} %fusion.60), channel_id=1, source_target_pairs={{1,0},{2,1},{3,2},{4,3},{5,4},{6,5},{7,6},{8,7},{9,8},{10,9},{11,1... | collective-permute-start | bytes 786440 | tf_op jit(solution)/shard_map/ppermute | solution.py:16
  46.8 14.3 %copy-start.9 = (bf16[128,1024]{1,0:T(8,128)(2,1)}, bf16[128,1024]{1,0:T(8,128)(2,1)S(1)}, u32[]{:S(2)}) copy-start(bf16[128,1024]{1,0:T(8,128)(2,1)S(1)} %collective-permute-done) | copy-start | bytes 786436
  46.8 5.9 %collective-permute-start.1 = (bf16[128,1024]{1,0:T(8,128)(2,1)S(1)}, bf16[128,1024]{1,0:T(8,128)(2,1)}, u32[]{:S(2)}, u32[]{:S(2)}) collective-permute-start(bf16[128,1024]{1,0:T(8,128)(2,1)S(1)} %collective-permute-done), channel_id=1, source_target_pairs={{0,1},{1,2},{2,3},{3,4},{4,5},{5,6},{6,7},{7,8},{8,9},{9,10},{10,1... | collective-permute-start | bytes 786440 | tf_op jit(solution)/shard_map/ppermute | solution.py:16
  51.4 9.7 %copy-start.7 = (bf16[128,1024]{1,0:T(8,128)(2,1)}, bf16[128,1024]{1,0:T(8,128)(2,1)S(1)}, u32[]{:S(2)}) copy-start(bf16[128,1024]{1,0:T(8,128)(2,1)S(1)} %collective-permute-done.4) | copy-start | bytes 786436
  51.4 8.4 %collective-permute-start.5 = (bf16[128,1024]{1,0:T(8,128)(2,1)S(1)}, bf16[128,1024]{1,0:T(8,128)(2,1)}, u32[]{:S(2)}, u32[]{:S(2)}) collective-permute-start(bf16[128,1024]{1,0:T(8,128)(2,1)S(1)} %collective-permute-done.4), channel_id=1, source_target_pairs={{1,0},{2,1},{3,2},{4,3},{5,4},{6,5},{7,6},{8,7},{9,8},{10,9},{11,1... | collective-permute-start | bytes 786440 | tf_op jit(solution)/shard_map/ppermute | solution.py:16
  52.7 8.4 %collective-permute-start.2 = (bf16[128,1024]{1,0:T(8,128)(2,1)}, bf16[128,1024]{1,0:T(8,128)(2,1)}, u32[]{:S(2)}, u32[]{:S(2)}) collective-permute-start(bf16[128,1024]{1,0:T(8,128)(2,1)} %collective-permute-done.1), channel_id=1, source_target_pairs={{0,1},{1,2},{2,3},{3,4},{4,5},{5,6},{6,7},{7,8},{8,9},{9,10},{10,1... | collective-permute-start | bytes 786440 | tf_op jit(solution)/shard_map/ppermute | solution.py:16
  59.8 12.1 %collective-permute-start.6 = (bf16[128,1024]{1,0:T(8,128)(2,1)}, bf16[128,1024]{1,0:T(8,128)(2,1)}, u32[]{:S(2)}, u32[]{:S(2)}) collective-permute-start(bf16[128,1024]{1,0:T(8,128)(2,1)} %collective-permute-done.5), channel_id=1, source_target_pairs={{1,0},{2,1},{3,2},{4,3},{5,4},{6,5},{7,6},{8,7},{9,8},{10,9},{11,1... | collective-permute-start | bytes 786440 | tf_op jit(solution)/shard_map/ppermute | solution.py:16
  61.1 12.0 %collective-permute-start.3 = (bf16[128,1024]{1,0:T(8,128)(2,1)}, bf16[128,1024]{1,0:T(8,128)(2,1)}, u32[]{:S(2)}, u32[]{:S(2)}) collective-permute-start(bf16[128,1024]{1,0:T(8,128)(2,1)} %collective-permute-done.2), channel_id=1, source_target_pairs={{0,1},{1,2},{2,3},{3,4},{4,5},{5,6},{6,7},{7,8},{8,9},{9,10},{10,1... | collective-permute-start | bytes 786440 | tf_op jit(solution)/shard_map/ppermute | solution.py:16
  71.9 15.8 %collective-permute-start.7 = (bf16[128,1024]{1,0:T(8,128)(2,1)}, bf16[128,1024]{1,0:T(8,128)(2,1)S(1)}, u32[]{:S(2)}, u32[]{:S(2)}) collective-permute-start(bf16[128,1024]{1,0:T(8,128)(2,1)} %collective-permute-done.6), channel_id=1, source_target_pairs={{1,0},{2,1},{3,2},{4,3},{5,4},{6,5},{7,6},{8,7},{9,8},{10,9},{11,1... | collective-permute-start | bytes 786440 | tf_op jit(solution)/shard_map/ppermute | solution.py:16
  73.2 9.4 %slice-start = ((s8[6291456]{0:T(1024)(128)(4,1)}), s8[4194304]{0:T(1024)(128)(4,1)S(1)}, s32[]{:S(2)}) async-start(s8[6291456]{0:T(1024)(128)(4,1)} %bitcast.101), calls=%async_computation.5 | async-start | bytes 8388608
  76.3 6.2 %slice-start.1 = ((s8[6291456]{0:T(1024)(128)(4,1)}), s8[2097152]{0:T(1024)(128)(4,1)S(1)}, s32[]{:S(2)}) async-start(s8[6291456]{0:T(1024)(128)(4,1)} %bitcast.101), calls=%async_computation.6 | async-start | bytes 4194304
  76.3 6.2 %copy-start.10 = (bf16[128,1024]{1,0:T(8,128)(2,1)S(1)}, bf16[128,1024]{1,0:T(8,128)(2,1)}, u32[]{:S(2)}) copy-start(bf16[128,1024]{1,0:T(8,128)(2,1)} %copy-done.9) | copy-start | bytes 786436
  82.5 1.0 copy-start.8
  88.4 2.1 copy-start.3
  95.2 8.4 %copy-start.4 = (bf16[128,1024]{0,1:T(8,128)(2,1)S(1)}, bf16[128,1024]{0,1:T(8,128)(2,1)}, u32[]{:S(2)}) copy-start(bf16[128,1024]{0,1:T(8,128)(2,1)} %copy.27) | copy-start | bytes 786436
  109.1 4.2 %copy-start.2 = (bf16[128,1024]{1,0:T(8,128)(2,1)S(1)}, bf16[128,1024]{1,0:T(8,128)(2,1)}, u32[]{:S(2)}) copy-start(bf16[128,1024]{1,0:T(8,128)(2,1)} %param.15) | copy-start | bytes 786436
  126.0 4.6 %copy-start.5 = (bf16[128,1024]{0,1:T(8,128)(2,1)S(1)}, bf16[128,1024]{0,1:T(8,128)(2,1)}, u32[]{:S(2)}) copy-start(bf16[128,1024]{0,1:T(8,128)(2,1)} %copy.27) | copy-start | bytes 786436
  190.1 2.1 copy-start.1
  193.8 22.8 %collective-permute-start.8 = (bf16[128,2048]{1,0:T(8,128)(2,1)S(1)}, bf16[128,2048]{1,0:T(8,128)(2,1)}, u32[]{:S(2)}, u32[]{:S(2)}) collective-permute-start(bf16[128,2048]{1,0:T(8,128)(2,1)S(1)} %get-tuple-element.8), channel_id=1, source_target_pairs={{0,1},{1,2},{2,3},{3,4},{4,5},{5,6},{6,7},{7,8},{8,9},{9,10},{10,1... | collective-permute-start | bytes 1572872 | tf_op jit(solution)/shard_map/ppermute | solution.py:16
  199.3 19.2 %collective-permute-start.15 = (bf16[128,2048]{1,0:T(8,128)(2,1)S(1)}, bf16[128,2048]{1,0:T(8,128)(2,1)}, u32[]{:S(2)}, u32[]{:S(2)}) collective-permute-start(bf16[128,2048]{1,0:T(8,128)(2,1)S(1)} %get-tuple-element.9), channel_id=1, source_target_pairs={{4,0},{5,1},{6,2},{7,3},{8,4},{9,5},{10,6},{11,7},{12,8},{13,9},{1... | collective-permute-start | bytes 1572872 | tf_op jit(solution)/shard_map/ppermute | solution.py:16
  200.5 22.8 %collective-permute-start.14 = (bf16[128,2048]{1,0:T(8,128)(2,1)S(1)}, bf16[128,2048]{1,0:T(8,128)(2,1)}, u32[]{:S(2)}, u32[]{:S(2)}) collective-permute-start(bf16[128,2048]{1,0:T(8,128)(2,1)S(1)} %get-tuple-element.10), channel_id=1, source_target_pairs={{0,4},{1,5},{2,6},{3,7},{4,8},{5,9},{6,10},{7,11},{8,12},{9,13},{1... | collective-permute-start | bytes 1572872 | tf_op jit(solution)/shard_map/ppermute | solution.py:16
  208.3 35.6 %collective-permute-start.13 = (bf16[128,2048]{1,0:T(8,128)(2,1)}, bf16[128,2048]{1,0:T(8,128)(2,1)}, u32[]{:S(2)}, u32[]{:S(2)}) collective-permute-start(bf16[128,2048]{1,0:T(8,128)(2,1)} %get-tuple-element.11), channel_id=1, source_target_pairs={{3,0},{4,1},{5,2},{6,3},{7,4},{8,5},{9,6},{10,7},{11,8},{12,9},{13... | collective-permute-start | bytes 1572872 | tf_op jit(solution)/shard_map/ppermute | solution.py:16
  209.8 35.9 %collective-permute-start.12 = (bf16[128,2048]{1,0:T(8,128)(2,1)}, bf16[128,2048]{1,0:T(8,128)(2,1)}, u32[]{:S(2)}, u32[]{:S(2)}) collective-permute-start(bf16[128,2048]{1,0:T(8,128)(2,1)} %get-tuple-element.12), channel_id=1, source_target_pairs={{0,3},{1,4},{2,5},{3,6},{4,7},{5,8},{6,9},{7,10},{8,11},{9,12},{10... | collective-permute-start | bytes 1572872 | tf_op jit(solution)/shard_map/ppermute | solution.py:16
  216.6 29.2 %collective-permute-start.11 = (bf16[128,2048]{1,0:T(8,128)(2,1)}, bf16[128,2048]{1,0:T(8,128)(2,1)}, u32[]{:S(2)}, u32[]{:S(2)}) collective-permute-start(bf16[128,2048]{1,0:T(8,128)(2,1)} %get-tuple-element.13), channel_id=1, source_target_pairs={{2,0},{3,1},{4,2},{5,3},{6,4},{7,5},{8,6},{9,7},{10,8},{11,9},{12,... | collective-permute-start | bytes 1572872 | tf_op jit(solution)/shard_map/ppermute | solution.py:16
  218.4 36.5 %collective-permute-start.10 = (bf16[128,2048]{1,0:T(8,128)(2,1)}, bf16[128,2048]{1,0:T(8,128)(2,1)}, u32[]{:S(2)}, u32[]{:S(2)}) collective-permute-start(bf16[128,2048]{1,0:T(8,128)(2,1)} %get-tuple-element.14), channel_id=1, source_target_pairs={{0,2},{1,3},{2,4},{3,5},{4,6},{5,7},{6,8},{7,9},{8,10},{9,11},{10,... | collective-permute-start | bytes 1572872 | tf_op jit(solution)/shard_map/ppermute | solution.py:16
  223.3 31.6 %collective-permute-start.9 = (bf16[128,2048]{1,0:T(8,128)(2,1)}, bf16[128,2048]{1,0:T(8,128)(2,1)}, u32[]{:S(2)}, u32[]{:S(2)}) collective-permute-start(bf16[128,2048]{1,0:T(8,128)(2,1)} %get-tuple-element.15), channel_id=1, source_target_pairs={{1,0},{2,1},{3,2},{4,3},{5,4},{6,5},{7,6},{8,7},{9,8},{10,9},{11,1... | collective-permute-start | bytes 1572872 | tf_op jit(solution)/shard_map/ppermute | solution.py:16
  243.7 14.3 %copy-start.6 = (f32[1024]{0:T(1024)S(1)}, f32[1024]{0:T(1024)}, u32[]{:S(2)}) copy-start(f32[1024]{0:T(1024)} %param.12) | copy-start | bytes 12292
  265.0 40.7 %all-to-all-start.2 = ((bf16[16,8,1024]{2,1,0:T(8,128)(2,1)}), bf16[16,8,1024]{2,1,0:T(8,128)(2,1)S(1)}, u32[]{:S(2)}, u32[]{:S(2)}) async-start(bf16[16,8,1024]{2,1,0:T(8,128)(2,1)} %bitcast.33), calls=%async_computation.2 | async-start | bytes 524288 | tf_op jit(solution)/shard_map/all_to_all | solution.py:130
Sparse Core Ops, SparseCore 0:
  116.1 78.6 reduce-scatter.1
where the time goes:
time: 318 us; the launch traced here: 316 us
  matrix products  85.6 us (27%)
  blocking collectives  60.1 us (19%)
  starting transfers between devices  59.4 us (19%)
  local copies, waits for them, and re-layouts  50.4 us (16%)
  other arithmetic  33.8 us (11%)
  between operations  15.2 us (5%)
  waiting for transfers between devices  11.6 us (4%)
    ppermute x16, starting transfers between devices, from_behind(): return lax.ppermute(block, axis, route)  54.3 us
    psum x1, blocking collectives, per_device(): grad_gain = lax.psum(gain_term, 'ctx') * norm_scale  33.8 us
    dot_general x1, matrix products, per_device(): jnp.einsum('shqk,sqhd->skhd', d_scores, heads_q, preferred_element_type=j...  19.2 us
    dot_general x1, matrix products, per_device(): jnp.einsum('shqk,skhd->sqhd', d_scores, heads_k, preferred_element_type=j...  19.1 us
    dot_general x8, matrix products, per_device(): jnp.dot(remote_piece, kv_weight, preferred_element_type=jnp.float32)  14.8 us
    all_to_all x1, blocking collectives, per_device(): lax.all_to_all(wanted, 'ctx', split_axis=0, concat_axis=0, tiled=True)  13.6 us
    all_to_all x1, blocking collectives, per_device(): lax.all_to_all(outgoing, 'ctx', split_axis=0, concat_axis=0, tiled=True)  12.6 us
    scatter-add x1, other arithmetic, per_device(): jnp.zeros(window_blocks.shape, jnp.float32).at[slot_index.reshape(-1)]  11.9 us
  transfers between devices with their start and end apart: 18, of which 3 were waited for; matrix products, arithmetic and copies ran while one was open for 40% of the time, Pallas kernels for 0%

commit v1 on v0

--- a/solution.py
+++ b/solution.py
@@ -118,7 +118,7 @@
     d_proj = jnp.concatenate([d_query, d_kv], axis=-1)
     d_normed = jnp.dot(d_proj, w_qkv.T, preferred_element_type=jnp.float32)
     gain_term = jnp.sum(d_normed * ordered_f * inv_rms, axis=0)
-    grad_gain = lax.psum(gain_term, "ctx") * norm_scale
+    grad_gain = jnp.sum(lax.all_gather(gain_term, "ctx"), axis=0) * norm_scale
     scaled = d_normed * norm_gain
     d_ordered = (
         cotangent.astype(jnp.float32)

time: 318 us -> 306 us (0.962)
  blocking collectives: 60.1 us -> 48.1 us
    psum x1 -> x0, blocking collectives: 33.8 us -> none  [per_device(): grad_gain = lax.psum(gain_term, 'ctx') * norm_scale]
    all_gather x0 -> x1, blocking collectives: none -> 21.9 us  [per_device(): grad_gain = jnp.sum(lax.all_gather(gain_term, 'ctx'), axis=0) * norm_scale]
  transfers between devices with their start and end apart: 18 -> 18, of which waited for: 3 -> 3; matrix products, arithmetic and copies ran while one was open for 40% -> 42% of each run, Pallas kernels for 0% -> 0%
where the time goes in v1:
time: 306 us; the launch traced here: 304 us
  matrix products  85.6 us (28%)
  starting transfers between devices  59.4 us (19%)
  local copies, waits for them, and re-layouts  50.4 us (16%)
  blocking collectives  48.1 us (16%)
  other arithmetic  33.8 us (11%)
  between operations  15.2 us (5%)
  waiting for transfers between devices  11.6 us (4%)
    ppermute x16, starting transfers between devices, from_behind(): return lax.ppermute(block, axis, route)  54.3 us
    all_gather x1, blocking collectives, per_device(): grad_gain = jnp.sum(lax.all_gather(gain_term, 'ctx'), axis=0) * norm_scale  21.9 us
    dot_general x1, matrix products, per_device(): jnp.einsum('shqk,sqhd->skhd', d_scores, heads_q, preferred_element_type=j...  19.2 us
    dot_general x1, matrix products, per_device(): jnp.einsum('shqk,skhd->sqhd', d_scores, heads_k, preferred_element_type=j...  19.1 us
    dot_general x8, matrix products, per_device(): jnp.dot(remote_piece, kv_weight, preferred_element_type=jnp.float32)  14.8 us
    all_to_all x1, blocking collectives, per_device(): lax.all_to_all(wanted, 'ctx', split_axis=0, concat_axis=0, tiled=True)  13.6 us
    all_to_all x1, blocking collectives, per_device(): lax.all_to_all(outgoing, 'ctx', split_axis=0, concat_axis=0, tiled=True)  12.6 us
    scatter-add x1, other arithmetic, per_device(): jnp.zeros(window_blocks.shape, jnp.float32).at[slot_index.reshape(-1)]  11.9 us
  transfers between devices with their start and end apart: 18, of which 3 were waited for; matrix products, arithmetic and copies ran while one was open for 42% of the time, Pallas kernels for 0%

profile of v1, /device:TPU:0, one launch (start us, length us, event | category | flops | bytes accessed | tf_op | source)
XLA Modules:
  0.0 304.1 jit_solution(10321079200044107415)
XLA Ops:
  11.9 13.6 %all_to_all.19 = s32[16,1,8]{2,1,0:T(1,128)S(1)} all-to-all(s32[16,1,8]{2,1,0:T(1,128)S(1)} %bitcast.117), channel_id=1, replica_groups=mesh['groups'=2,'ctx'=16] {'ctx'}, dimensions={0} | all-to-all | bytes 1024 | tf_op jit(solution)/shard_map/all_to_all | solution.py:48
  28.9 12.6 %all_to_all.20 = bf16[16,8,1024]{2,1,0:T(8,128)(2,1)S(1)} all-to-all(bf16[16,8,1024]{2,1,0:T(8,128)(2,1)S(1)} %bitcast.109), channel_id=1, replica_groups=mesh['groups'=2,'ctx'=16] {'ctx'}, dimensions={0} | all-to-all | bytes 524288 | tf_op jit(solution)/shard_map/all_to_all | solution.py:51
  46.8 4.6 %collective-permute-start.1 = (bf16[128,1024]{1,0:T(8,128)(2,1)S(1)}, bf16[128,1024]{1,0:T(8,128)(2,1)}, u32[]{:S(2)}, u32[]{:S(2)}) collective-permute-start(bf16[128,1024]{1,0:T(8,128)(2,1)S(1)} %collective-permute-done), channel_id=1, source_target_pairs={{0,1},{1,2},{2,3},{3,4},{4,5},{5,6},{6,7},{7,8},{8,9},{9,10},{10,1... | collective-permute-start | bytes 786440 | tf_op jit(solution)/shard_map/ppermute | solution.py:16
  52.7 6.4 %collective-permute-start.2 = (bf16[128,1024]{1,0:T(8,128)(2,1)}, bf16[128,1024]{1,0:T(8,128)(2,1)}, u32[]{:S(2)}, u32[]{:S(2)}) collective-permute-start(bf16[128,1024]{1,0:T(8,128)(2,1)} %collective-permute-done.1), channel_id=1, source_target_pairs={{0,1},{1,2},{2,3},{3,4},{4,5},{5,6},{6,7},{7,8},{8,9},{9,10},{10,1... | collective-permute-start | bytes 786440 | tf_op jit(solution)/shard_map/ppermute | solution.py:16
  61.1 6.1 %collective-permute-start.3 = (bf16[128,1024]{1,0:T(8,128)(2,1)}, bf16[128,1024]{1,0:T(8,128)(2,1)}, u32[]{:S(2)}, u32[]{:S(2)}) collective-permute-start(bf16[128,1024]{1,0:T(8,128)(2,1)} %collective-permute-done.2), channel_id=1, source_target_pairs={{0,1},{1,2},{2,3},{3,4},{4,5},{5,6},{6,7},{7,8},{8,9},{9,10},{10,1... | collective-permute-start | bytes 786440 | tf_op jit(solution)/shard_map/ppermute | solution.py:16
  67.2 3.8 %convolution_convert_fusion = bf16[128,3072]{1,0:T(8,128)(2,1)S(1)} fusion(bf16[128,1024]{1,0:T(8,128)(2,1)S(1)} %fusion.60, bf16[1024,3072]{1,0:T(8,128)(2,1)} %param.13), kind=kOutput, calls=%fused_computation.16 | convolution fusion | flops 805699584 | bytes 7340032 | tf_op jit(solution)/shard_map/dot_general | solution.py:58
  73.2 3.1 %fusion.24 = bf16[1152,2048]{1,0:T(8,128)(2,1)S(1)} fusion(bf16[128,1024]{1,0:T(8,128)(2,1)} %collective-permute-done.3, bf16[1024,3072]{1,0:T(8,128)(2,1)} %param.13), kind=kOutput, calls=%fused_computation.40 | convolution fusion | flops 537133056 | bytes 4980736 | tf_op jit(solution)/shard_map/dot_general | solution.py:72
  76.3 3.1 %fusion.23 = bf16[1152,2048]{1,0:T(8,128)(2,1)S(1)} fusion(bf16[1152,2048]{1,0:T(8,128)(2,1)S(1)} %fusion.24, bf16[128,1024]{1,0:T(8,128)(2,1)} %collective-permute-done.2, bf16[1024,3072]{1,0:T(8,128)(2,1)} %param.13), kind=kOutput, calls=%fused_computation.38 | convolution fusion | flops 537133056 | bytes 4980736 | tf_op jit(solution)/shard_map/dot_general | solution.py:72
  90.5 4.7 %gather_fusion.2 = bf16[5,128,2048]{2,1,0:T(8,128)(2,1)} fusion(bf16[9,128,2048]{2,1,0:T(8,128)(2,1)} %bitcast.106, s32[1024]{0:T(1024)S(1)} %pad_clamp_fusion), kind=kCustom, calls=%fused_computation.2 | custom fusion | bytes 5242900 | tf_op jit(solution)/shard_map/gather | solution.py:82
  95.2 3.5 %fusion.89 = (bf16[1,640,1024]{2,1,0:T(8,128)(2,1)}, bf16[1,640,1024]{2,1,0:T(8,128)(2,1)}) fusion(bf16[1,640,2048]{2,1,0:T(8,128)(2,1)} %bitcast.103), kind=kLoop, calls=%fused_computation.138 | loop fusion | bytes 5242880 | tf_op jit(solution)/shard_map/slice | solution.py:83
  103.6 5.5 %fusion.90 = (f32[16,128]{1,0:T(8,128)S(1)}, f32[16,128,640]{2,1,0:T(8,128)}) fusion(pred[640]{0:T(1024)(128)(4,1)S(1)} %fusion.75, bf16[128,16,64]{0,2,1:T(8,128)(2,1)S(1)} %bitcast.114, bf16[640,16,64]{0,2,1:T(8,128)(2,1)} %bitcast.107), kind=kOutput, calls=%fused_computation.139 | convolution fusion | flops 173015680 | bytes 6824576 | tf_op jit(solution)/shard_map/sub | solution.py:28
  109.2 4.1 %fusion.31 = bf16[16,64,128]{2,1,0:T(8,128)(2,1)S(1)} fusion(bf16[640,16,64]{0,2,1:T(8,128)(2,1)} %bitcast.104, f32[16,128,640]{2,1,0:T(8,128)} %get-tuple-element.23, f32[16,128]{1,0:T(8,128)S(1)} %get-tuple-element.22), kind=kOutput, calls=%fused_computation.47 | convolution fusion | flops 170524672 | bytes 6823936 | tf_op jit(solution)/shard_map/shqk,skhd->sqhd/dot_general | solution.py:88
  117.0 4.6 %convolution_bitcast_fusion = f32[1,640,16,64]{1,3,2,0:T(8,128)} fusion(bf16[128,16,64]{0,2,1:T(8,128)(2,1)S(1)} %bitcast.112, f32[16,128,640]{2,1,0:T(8,128)} %get-tuple-element.23, f32[16,128]{1,0:T(8,128)S(1)} %get-tuple-element.22), kind=kOutput, calls=%fused_computation.42 | convolution fusion | flops 170393600 | bytes 8134656 | tf_op jit(solution)/shard_map/shqk,sqhd->skhd/dot_general | solution.py:103
  121.6 4.4 %reshape.226 = f32[5,128,1024]{1,0,2:T(8,128)} reshape(f32[1,640,16,64]{1,3,2,0:T(8,128)} %convolution_bitcast_fusion) | data formatting | bytes 5242880 | tf_op jit(solution)/shard_map/reshape | solution.py:105
  126.0 4.6 %fusion.91 = f32[16,128,640]{2,1,0:T(8,128)} fusion(bf16[128,16,64]{0,2,1:T(8,128)(2,1)S(1)} %bitcast.113, bf16[640,16,64]{0,2,1:T(8,128)(2,1)} %bitcast.105), kind=kOutput, calls=%fused_computation.140 | convolution fusion | flops 167772160 | bytes 6815744 | tf_op jit(solution)/shard_map/sqhd,skhd->shqk/dot_general | solution.py:97
  130.6 19.2 %fusion.25 = f32[1,640,16,64]{1,3,2,0:T(8,128)} fusion(bf16[128,16,64]{0,2,1:T(8,128)(2,1)S(1)} %bitcast.115, f32[16,128,640]{2,1,0:T(8,128)} %fusion.91, f32[16,128,640]{2,1,0:T(8,128)} %get-tuple-element.23, f32[16,128]{1,0:T(8,128)S(1)} %get-tuple-element.22), kind=kOutput, calls=%fused_computation.41 | convolution fusion | flops 176949888 | bytes 13377536 | tf_op jit(solution)/shard_map/shqk,sqhd->skhd/dot_general | solution.py:102
  149.9 4.4 %reshape.225 = f32[5,128,1024]{1,0,2:T(8,128)} reshape(f32[1,640,16,64]{1,3,2,0:T(8,128)} %fusion.25) | data formatting | bytes 5242880 | tf_op jit(solution)/shard_map/reshape | solution.py:105
  154.3 6.7 %pad_maximum_fusion = f32[5,128,2048]{1,0,2:T(8,128)} fusion(f32[5,128,1024]{1,0,2:T(8,128)} %reshape.226, f32[5,128,1024]{1,0,2:T(8,128)} %reshape.225), kind=kLoop, calls=%fused_computation.9 | loop fusion | flops 1310720 | bytes 10485760 | tf_op jit(solution)/shard_map/concatenate | solution.py:104
  161.0 7.9 %copy.37 = f32[5,128,2048]{2,1,0:T(8,128)} copy(f32[5,128,2048]{1,0,2:T(8,128)} %pad_maximum_fusion) | data formatting | bytes 10485760 | tf_op jit(solution)/shard_map/concatenate | solution.py:104
  168.9 4.8 %broadcast_in_dim.22 = f32[9,128,2048]{2,1,0:T(8,128)} broadcast(f32[]{:T(128)} %constant.63.clone.1), dimensions={} | broadcast | bytes 9437188 | tf_op jit(solution)/shard_map/broadcast_in_dim | solution.py:107
  173.7 11.9 %scatter_fusion = f32[9,128,2048]{2,1,0:T(8,128)} fusion(f32[9,128,2048]{2,1,0:T(8,128)} %broadcast_in_dim.22, s32[5]{0:T(128)S(1)} %fusion.81, f32[5,128,2048]{2,1,0:T(8,128)} %copy.37), kind=kCustom, calls=%fused_computation.5 | custom fusion | flops 1310720 | bytes 15728660 | tf_op jit(solution)/shard_map/scatter-add | solution.py:107
  185.7 4.4 %convert_element_type.137 = bf16[9,128,2048]{2,1,0:T(8,128)(2,1)S(1)} convert(f32[9,128,2048]{2,1,0:T(8,128)} %scatter_fusion) | non-fusion elementwise | flops 2359296 | bytes 14155776 | tf_op jit(solution)/shard_map/convert_element_type | solution.py:108
  193.8 5.4 %collective-permute-start.8 = (bf16[128,2048]{1,0:T(8,128)(2,1)S(1)}, bf16[128,2048]{1,0:T(8,128)(2,1)}, u32[]{:S(2)}, u32[]{:S(2)}) collective-permute-start(bf16[128,2048]{1,0:T(8,128)(2,1)S(1)} %get-tuple-element.8), channel_id=1, source_target_pairs={{0,1},{1,2},{2,3},{3,4},{4,5},{5,6},{6,7},{7,8},{8,9},{9,10},{10,1... | collective-permute-start | bytes 1572872 | tf_op jit(solution)/shard_map/ppermute | solution.py:16
  200.5 7.8 %collective-permute-start.14 = (bf16[128,2048]{1,0:T(8,128)(2,1)S(1)}, bf16[128,2048]{1,0:T(8,128)(2,1)}, u32[]{:S(2)}, u32[]{:S(2)}) collective-permute-start(bf16[128,2048]{1,0:T(8,128)(2,1)S(1)} %get-tuple-element.10), channel_id=1, source_target_pairs={{0,4},{1,5},{2,6},{3,7},{4,8},{5,9},{6,10},{7,11},{8,12},{9,13},{1... | collective-permute-start | bytes 1572872 | tf_op jit(solution)/shard_map/ppermute | solution.py:16
  209.8 6.8 %collective-permute-start.12 = (bf16[128,2048]{1,0:T(8,128)(2,1)}, bf16[128,2048]{1,0:T(8,128)(2,1)}, u32[]{:S(2)}, u32[]{:S(2)}) collective-permute-start(bf16[128,2048]{1,0:T(8,128)(2,1)} %get-tuple-element.12), channel_id=1, source_target_pairs={{0,3},{1,4},{2,5},{3,6},{4,7},{5,8},{6,9},{7,10},{8,11},{9,12},{10... | collective-permute-start | bytes 1572872 | tf_op jit(solution)/shard_map/ppermute | solution.py:16
  218.4 4.9 %collective-permute-start.10 = (bf16[128,2048]{1,0:T(8,128)(2,1)}, bf16[128,2048]{1,0:T(8,128)(2,1)}, u32[]{:S(2)}, u32[]{:S(2)}) collective-permute-start(bf16[128,2048]{1,0:T(8,128)(2,1)} %get-tuple-element.14), channel_id=1, source_target_pairs={{0,2},{1,3},{2,4},{3,5},{4,6},{5,7},{6,8},{7,9},{8,10},{9,11},{10,... | collective-permute-start | bytes 1572872 | tf_op jit(solution)/shard_map/ppermute | solution.py:16
  224.6 19.1 %fusion.34 = bf16[16,64,128]{2,1,0:T(8,128)(2,1)S(1)} fusion(bf16[640,16,64]{0,2,1:T(8,128)(2,1)} %bitcast.108, f32[16,128,640]{2,1,0:T(8,128)} %fusion.91, f32[16,128,640]{2,1,0:T(8,128)} %get-tuple-element.23, f32[16,128]{1,0:T(8,128)S(1)} %get-tuple-element.22), kind=kOutput, calls=%fused_computation.48 | convolution fusion | flops 177080960 | bytes 12066816 | tf_op jit(solution)/shard_map/shqk,skhd->sqhd/dot_general | solution.py:100
  245.8 9.2 %collective-permute-done.10 = bf16[128,2048]{1,0:T(8,128)(2,1)} collective-permute-done((bf16[128,2048]{1,0:T(8,128)(2,1)}, bf16[128,2048]{1,0:T(8,128)(2,1)}, u32[]{:S(2)}, u32[]{:S(2)}) %collective-permute-start.10) | collective-permute-done | bytes 524320 | tf_op jit(solution)/shard_map/ppermute | solution.py:16
  255.0 3.1 %fusion.45 = bf16[128,2048]{1,0:T(8,128)(2,1)S(1)} fusion(bf16[128,2048]{1,0:T(8,128)(2,1)} %collective-permute-done.15, bf16[128,2048]{1,0:T(8,128)(2,1)} %collective-permute-done.14, bf16[128,2048]{1,0:T(8,128)(2,1)} %collective-permute-done.13, bf16[128,2048]{1,0:T(8,128)(2,1)} %collective-permute-done.12, bf16[128,2048]{1,0:T(8,128)(2,1)} %collective-permute-done.11, ...), kind=kLoop, calls=%fused_computation.64 | loop fusion | flops 4718592 | bytes 5242880 | tf_op jit(solution)/shard_map/convert_element_type | solution.py:117
  258.0 5.1 %fusion.66 = (f32[1024]{0:T(1024)S(1)}, f32[128]{0:T(128)S(1)}, f32[128,1024]{1,0:T(8,128)S(1)}) fusion(bf16[128,1024]{1,0:T(8,128)(2,1)S(1)} %scatter_custom_fusion, f32[128]{0:T(128)S(1)} %get-tuple-element.19, f32[1024]{0:T(1024)S(1)} %copy-done.6, bf16[1024,3072]{1,0:T(8,128)(2,1)} %param.13, bf16[128,2048]{1,0:T(8,128)(2,1)S(1)} %fusion.45, ...), kind=kOutput, calls=%fused_computation.85 | convolution fusion | flops 807795584 | bytes 7873536 | tf_op jit(solution)/shard_map/dot_general | solution.py:119
  265.0 5.1 %all-to-all-start.2 = ((bf16[16,8,1024]{2,1,0:T(8,128)(2,1)}), bf16[16,8,1024]{2,1,0:T(8,128)(2,1)S(1)}, u32[]{:S(2)}, u32[]{:S(2)}) async-start(bf16[16,8,1024]{2,1,0:T(8,128)(2,1)} %bitcast.33), calls=%async_computation.2 | async-start | bytes 524288 | tf_op jit(solution)/shard_map/all_to_all | solution.py:130
  271.3 21.9 %all-gather = f32[16384]{0:T(1024)S(1)} all-gather(f32[1024]{0:T(1024)S(1)} %get-tuple-element.6), channel_id=2, replica_groups=mesh['groups'=2,'ctx'=16] {'ctx'}, dimensions={0}, use_global_device_ids=true | all-gather | bytes 69632 | tf_op jit(solution)/shard_map/all_gather | solution.py:121
  (103 shorter events, 56.3 us)
Async XLA Ops:
  7.2 108.8 %copy-start = (bf16[1024,1024]{1,0:T(8,128)(2,1)S(1)}, bf16[1024,1024]{1,0:T(8,128)(2,1)}, u32[]{:S(2)}) copy-start(bf16[1024,1024]{1,0:T(8,128)(2,1)} %param.14) | copy-start | bytes 6291460
  7.2 51.9 %copy-start.11 = (s32[1,5]{1,0:T(1,128)S(1)}, s32[1,5]{1,0:T(1,128)}, u32[]{:S(2)}) copy-start(s32[1,5]{1,0:T(1,128)} %param.10) | copy-start | bytes 64
  7.2 288.4 %reduce-scatter.2.cloned.1.call-start = ((), (), s32[]{:S(2)}) async-start(), calls=%async_computation.4 | async-start | bytes 4456448 | tf_op jit(solution)/shard_map/reduce_scatter | solution.py:137
  43.7 3.1 %collective-permute-start = (bf16[128,1024]{1,0:T(8,128)(2,1)S(1)}, bf16[128,1024]{1,0:T(8,128)(2,1)S(1)}, u32[]{:S(2)}, u32[]{:S(2)}) collective-permute-start(bf16[128,1024]{1,0:T(8,128)(2,1)S(1)} %fusion.60), channel_id=1, source_target_pairs={{0,1},{1,2},{2,3},{3,4},{4,5},{5,6},{6,7},{7,8},{8,9},{9,10},{10,1... | collective-permute-start | bytes 786440 | tf_op jit(solution)/shard_map/ppermute | solution.py:16
  45.5 5.9 %collective-permute-start.4 = (bf16[128,1024]{1,0:T(8,128)(2,1)S(1)}, bf16[128,1024]{1,0:T(8,128)(2,1)S(1)}, u32[]{:S(2)}, u32[]{:S(2)}) collective-permute-start(bf16[128,1024]{1,0:T(8,128)(2,1)S(1)} %fusion.60), channel_id=1, source_target_pairs={{1,0},{2,1},{3,2},{4,3},{5,4},{6,5},{7,6},{8,7},{9,8},{10,9},{11,1... | collective-permute-start | bytes 786440 | tf_op jit(solution)/shard_map/ppermute | solution.py:16
  46.8 14.3 %copy-start.9 = (bf16[128,1024]{1,0:T(8,128)(2,1)}, bf16[128,1024]{1,0:T(8,128)(2,1)S(1)}, u32[]{:S(2)}) copy-start(bf16[128,1024]{1,0:T(8,128)(2,1)S(1)} %collective-permute-done) | copy-start | bytes 786436
  46.8 5.9 %collective-permute-start.1 = (bf16[128,1024]{1,0:T(8,128)(2,1)S(1)}, bf16[128,1024]{1,0:T(8,128)(2,1)}, u32[]{:S(2)}, u32[]{:S(2)}) collective-permute-start(bf16[128,1024]{1,0:T(8,128)(2,1)S(1)} %collective-permute-done), channel_id=1, source_target_pairs={{0,1},{1,2},{2,3},{3,4},{4,5},{5,6},{6,7},{7,8},{8,9},{9,10},{10,1... | collective-permute-start | bytes 786440 | tf_op jit(solution)/shard_map/ppermute | solution.py:16
  51.4 9.7 %copy-start.7 = (bf16[128,1024]{1,0:T(8,128)(2,1)}, bf16[128,1024]{1,0:T(8,128)(2,1)S(1)}, u32[]{:S(2)}) copy-start(bf16[128,1024]{1,0:T(8,128)(2,1)S(1)} %collective-permute-done.4) | copy-start | bytes 786436
  51.4 8.4 %collective-permute-start.5 = (bf16[128,1024]{1,0:T(8,128)(2,1)S(1)}, bf16[128,1024]{1,0:T(8,128)(2,1)}, u32[]{:S(2)}, u32[]{:S(2)}) collective-permute-start(bf16[128,1024]{1,0:T(8,128)(2,1)S(1)} %collective-permute-done.4), channel_id=1, source_target_pairs={{1,0},{2,1},{3,2},{4,3},{5,4},{6,5},{7,6},{8,7},{9,8},{10,9},{11,1... | collective-permute-start | bytes 786440 | tf_op jit(solution)/shard_map/ppermute | solution.py:16
  52.7 8.4 %collective-permute-start.2 = (bf16[128,1024]{1,0:T(8,128)(2,1)}, bf16[128,1024]{1,0:T(8,128)(2,1)}, u32[]{:S(2)}, u32[]{:S(2)}) collective-permute-start(bf16[128,1024]{1,0:T(8,128)(2,1)} %collective-permute-done.1), channel_id=1, source_target_pairs={{0,1},{1,2},{2,3},{3,4},{4,5},{5,6},{6,7},{7,8},{8,9},{9,10},{10,1... | collective-permute-start | bytes 786440 | tf_op jit(solution)/shard_map/ppermute | solution.py:16
  59.8 12.1 %collective-permute-start.6 = (bf16[128,1024]{1,0:T(8,128)(2,1)}, bf16[128,1024]{1,0:T(8,128)(2,1)}, u32[]{:S(2)}, u32[]{:S(2)}) collective-permute-start(bf16[128,1024]{1,0:T(8,128)(2,1)} %collective-permute-done.5), channel_id=1, source_target_pairs={{1,0},{2,1},{3,2},{4,3},{5,4},{6,5},{7,6},{8,7},{9,8},{10,9},{11,1... | collective-permute-start | bytes 786440 | tf_op jit(solution)/shard_map/ppermute | solution.py:16
  61.1 12.0 %collective-permute-start.3 = (bf16[128,1024]{1,0:T(8,128)(2,1)}, bf16[128,1024]{1,0:T(8,128)(2,1)}, u32[]{:S(2)}, u32[]{:S(2)}) collective-permute-start(bf16[128,1024]{1,0:T(8,128)(2,1)} %collective-permute-done.2), channel_id=1, source_target_pairs={{0,1},{1,2},{2,3},{3,4},{4,5},{5,6},{6,7},{7,8},{8,9},{9,10},{10,1... | collective-permute-start | bytes 786440 | tf_op jit(solution)/shard_map/ppermute | solution.py:16
  71.9 15.8 %collective-permute-start.7 = (bf16[128,1024]{1,0:T(8,128)(2,1)}, bf16[128,1024]{1,0:T(8,128)(2,1)S(1)}, u32[]{:S(2)}, u32[]{:S(2)}) collective-permute-start(bf16[128,1024]{1,0:T(8,128)(2,1)} %collective-permute-done.6), channel_id=1, source_target_pairs={{1,0},{2,1},{3,2},{4,3},{5,4},{6,5},{7,6},{8,7},{9,8},{10,9},{11,1... | collective-permute-start | bytes 786440 | tf_op jit(solution)/shard_map/ppermute | solution.py:16
  73.2 9.4 %slice-start = ((s8[6291456]{0:T(1024)(128)(4,1)}), s8[4194304]{0:T(1024)(128)(4,1)S(1)}, s32[]{:S(2)}) async-start(s8[6291456]{0:T(1024)(128)(4,1)} %bitcast.101), calls=%async_computation.5 | async-start | bytes 8388608
  76.3 6.2 %slice-start.1 = ((s8[6291456]{0:T(1024)(128)(4,1)}), s8[2097152]{0:T(1024)(128)(4,1)S(1)}, s32[]{:S(2)}) async-start(s8[6291456]{0:T(1024)(128)(4,1)} %bitcast.101), calls=%async_computation.6 | async-start | bytes 4194304
  76.3 6.2 %copy-start.10 = (bf16[128,1024]{1,0:T(8,128)(2,1)S(1)}, bf16[128,1024]{1,0:T(8,128)(2,1)}, u32[]{:S(2)}) copy-start(bf16[128,1024]{1,0:T(8,128)(2,1)} %copy-done.9) | copy-start | bytes 786436
  82.5 1.0 copy-start.8
  88.4 2.1 copy-start.3
  95.2 8.4 %copy-start.4 = (bf16[128,1024]{0,1:T(8,128)(2,1)S(1)}, bf16[128,1024]{0,1:T(8,128)(2,1)}, u32[]{:S(2)}) copy-start(bf16[128,1024]{0,1:T(8,128)(2,1)} %copy.34) | copy-start | bytes 786436
  109.1 4.2 %copy-start.2 = (bf16[128,1024]{1,0:T(8,128)(2,1)S(1)}, bf16[128,1024]{1,0:T(8,128)(2,1)}, u32[]{:S(2)}) copy-start(bf16[128,1024]{1,0:T(8,128)(2,1)} %param.15) | copy-start | bytes 786436
  126.0 4.6 %copy-start.5 = (bf16[128,1024]{0,1:T(8,128)(2,1)S(1)}, bf16[128,1024]{0,1:T(8,128)(2,1)}, u32[]{:S(2)}) copy-start(bf16[128,1024]{0,1:T(8,128)(2,1)} %copy.34) | copy-start | bytes 786436
  190.1 2.1 copy-start.1
  193.8 22.8 %collective-permute-start.8 = (bf16[128,2048]{1,0:T(8,128)(2,1)S(1)}, bf16[128,2048]{1,0:T(8,128)(2,1)}, u32[]{:S(2)}, u32[]{:S(2)}) collective-permute-start(bf16[128,2048]{1,0:T(8,128)(2,1)S(1)} %get-tuple-element.8), channel_id=1, source_target_pairs={{0,1},{1,2},{2,3},{3,4},{4,5},{5,6},{6,7},{7,8},{8,9},{9,10},{10,1... | collective-permute-start | bytes 1572872 | tf_op jit(solution)/shard_map/ppermute | solution.py:16
  199.3 19.2 %collective-permute-start.15 = (bf16[128,2048]{1,0:T(8,128)(2,1)S(1)}, bf16[128,2048]{1,0:T(8,128)(2,1)}, u32[]{:S(2)}, u32[]{:S(2)}) collective-permute-start(bf16[128,2048]{1,0:T(8,128)(2,1)S(1)} %get-tuple-element.9), channel_id=1, source_target_pairs={{4,0},{5,1},{6,2},{7,3},{8,4},{9,5},{10,6},{11,7},{12,8},{13,9},{1... | collective-permute-start | bytes 1572872 | tf_op jit(solution)/shard_map/ppermute | solution.py:16
  200.5 22.8 %collective-permute-start.14 = (bf16[128,2048]{1,0:T(8,128)(2,1)S(1)}, bf16[128,2048]{1,0:T(8,128)(2,1)}, u32[]{:S(2)}, u32[]{:S(2)}) collective-permute-start(bf16[128,2048]{1,0:T(8,128)(2,1)S(1)} %get-tuple-element.10), channel_id=1, source_target_pairs={{0,4},{1,5},{2,6},{3,7},{4,8},{5,9},{6,10},{7,11},{8,12},{9,13},{1... | collective-permute-start | bytes 1572872 | tf_op jit(solution)/shard_map/ppermute | solution.py:16
  208.3 35.6 %collective-permute-start.13 = (bf16[128,2048]{1,0:T(8,128)(2,1)}, bf16[128,2048]{1,0:T(8,128)(2,1)}, u32[]{:S(2)}, u32[]{:S(2)}) collective-permute-start(bf16[128,2048]{1,0:T(8,128)(2,1)} %get-tuple-element.11), channel_id=1, source_target_pairs={{3,0},{4,1},{5,2},{6,3},{7,4},{8,5},{9,6},{10,7},{11,8},{12,9},{13... | collective-permute-start | bytes 1572872 | tf_op jit(solution)/shard_map/ppermute | solution.py:16
  209.8 35.9 %collective-permute-start.12 = (bf16[128,2048]{1,0:T(8,128)(2,1)}, bf16[128,2048]{1,0:T(8,128)(2,1)}, u32[]{:S(2)}, u32[]{:S(2)}) collective-permute-start(bf16[128,2048]{1,0:T(8,128)(2,1)} %get-tuple-element.12), channel_id=1, source_target_pairs={{0,3},{1,4},{2,5},{3,6},{4,7},{5,8},{6,9},{7,10},{8,11},{9,12},{10... | collective-permute-start | bytes 1572872 | tf_op jit(solution)/shard_map/ppermute | solution.py:16
  216.6 29.2 %collective-permute-start.11 = (bf16[128,2048]{1,0:T(8,128)(2,1)}, bf16[128,2048]{1,0:T(8,128)(2,1)}, u32[]{:S(2)}, u32[]{:S(2)}) collective-permute-start(bf16[128,2048]{1,0:T(8,128)(2,1)} %get-tuple-element.13), channel_id=1, source_target_pairs={{2,0},{3,1},{4,2},{5,3},{6,4},{7,5},{8,6},{9,7},{10,8},{11,9},{12,... | collective-permute-start | bytes 1572872 | tf_op jit(solution)/shard_map/ppermute | solution.py:16
  218.4 36.5 %collective-permute-start.10 = (bf16[128,2048]{1,0:T(8,128)(2,1)}, bf16[128,2048]{1,0:T(8,128)(2,1)}, u32[]{:S(2)}, u32[]{:S(2)}) collective-permute-start(bf16[128,2048]{1,0:T(8,128)(2,1)} %get-tuple-element.14), channel_id=1, source_target_pairs={{0,2},{1,3},{2,4},{3,5},{4,6},{5,7},{6,8},{7,9},{8,10},{9,11},{10,... | collective-permute-start | bytes 1572872 | tf_op jit(solution)/shard_map/ppermute | solution.py:16
  223.3 31.6 %collective-permute-start.9 = (bf16[128,2048]{1,0:T(8,128)(2,1)}, bf16[128,2048]{1,0:T(8,128)(2,1)}, u32[]{:S(2)}, u32[]{:S(2)}) collective-permute-start(bf16[128,2048]{1,0:T(8,128)(2,1)} %get-tuple-element.15), channel_id=1, source_target_pairs={{1,0},{2,1},{3,2},{4,3},{5,4},{6,5},{7,6},{8,7},{9,8},{10,9},{11,1... | collective-permute-start | bytes 1572872 | tf_op jit(solution)/shard_map/ppermute | solution.py:16
  243.7 14.3 %copy-start.6 = (f32[1024]{0:T(1024)S(1)}, f32[1024]{0:T(1024)}, u32[]{:S(2)}) copy-start(f32[1024]{0:T(1024)} %param.12) | copy-start | bytes 12292
  265.0 28.8 %all-to-all-start.2 = ((bf16[16,8,1024]{2,1,0:T(8,128)(2,1)}), bf16[16,8,1024]{2,1,0:T(8,128)(2,1)S(1)}, u32[]{:S(2)}, u32[]{:S(2)}) async-start(bf16[16,8,1024]{2,1,0:T(8,128)(2,1)} %bitcast.33), calls=%async_computation.2 | async-start | bytes 524288 | tf_op jit(solution)/shard_map/all_to_all | solution.py:130
Sparse Core Ops, SparseCore 0:
  116.1 78.6 reduce-scatter.1
